TPU v7x, 32 devices: a whole 2x2x4 slice. The times are simulated.
32 devices in a mesh: groups: 1, samp: 4 (over x, core), var: 8 (over z, y).
Axes of the slice: x: 2, y: 2, z: 4, core: 2. Of those that a mesh axis runs over, the one named last changes fastest.
Arguments:
- expression: bfloat16 [4096, 5120], P(('groups', 'samp'), 'var'), may hold values from -6 to 6
- genotypes: bfloat16 [4096, 1536], P(('groups', 'samp'), 'var'), may hold values from 0 to 2
- covariates: bfloat16 [4096, 64], P(('groups', 'samp')), may hold values from -6 to 6
- distance_bins: int32 [24, 5120], P('groups', ('var', 'samp')), may hold values from 0 to 15
- gene_folds: int32 [5120], P(('groups', 'var', 'samp')), may hold values from 0 to 4
- fold_weights: float32 [5, 16], replicated, may hold values from 0.25 to 4
Outputs:
- weighted_stats: float32 [5120, 1536], P(('groups', 'var', 'samp'))
Inputs may be any that keep to these rules, and one draw needn't show every extreme that they name: `distance_bins`: bins index rows of fold_weights' second dimension. `gene_folds`: folds index rows of fold_weights.
All inputs are finite; a program needn't handle non-finite values.
Results may differ from a plain program's by a relative error of at most 0.0047.
Values may be sent and summed in bfloat16 or wider, within the bound.
A program may use at most 64 MiB of HBM per device.

v0:
```python
import jax
import jax.numpy as jnp
from jax import lax
from jax.sharding import PartitionSpec as P

COVS = 64
VARS = 1536
VTILE = 64
NBINS = 16
FOLDS = 5
VTILES = 24


def solve_fit(data, design, factor, cross):
    beta = jax.scipy.linalg.cho_solve((factor, True), cross)
    fitted = jnp.dot(design.astype(jnp.float32), beta, precision=lax.Precision.HIGHEST)
    return (beta, data.astype(jnp.float32) - fitted)


def shards(expression, genotypes, covariates, distance_bins, gene_folds, fold_weights):
    sample_rows = expression.shape[0]
    samples = sample_rows * lax.axis_size("samp")
    design = jnp.concatenate([jnp.ones((sample_rows, 1), jnp.bfloat16), covariates], axis=1)
    source = lax.all_gather(genotypes, "var", axis=1, tiled=True)
    gram = jnp.dot(design.T, design, preferred_element_type=jnp.float32)
    expr_cross = jnp.dot(design.T, expression, preferred_element_type=jnp.float32)
    geno_cross = jnp.dot(design.T, source, preferred_element_type=jnp.float32)
    partial_sums = (gram, expr_cross, geno_cross)
    summed = lax.psum((partial_sums[0], partial_sums[1], partial_sums[2]), "samp")
    gram, expr_cross, geno_cross = (summed[0], summed[1], summed[2])
    factor = jnp.linalg.cholesky(gram)
    expr_beta, expr_resid = solve_fit(expression, design, factor, expr_cross)
    geno_beta, geno_resid = solve_fit(source, design, factor, geno_cross)
    expr_norm, geno_norm = lax.psum(
        (jnp.sum(expr_resid * expr_resid, axis=0), jnp.sum(geno_resid * geno_resid, axis=0)), "samp"
    )
    expr_unit = (expr_resid * lax.rsqrt(expr_norm + 1e-06)).astype(jnp.bfloat16)
    geno_unit = (geno_resid * lax.rsqrt(geno_norm + 1e-06)).astype(jnp.bfloat16)
    terms = lax.dot_general(
        expr_unit, geno_unit, (((0,), (0,)), ((), ())), preferred_element_type=jnp.float32
    )
    corr = lax.psum_scatter(terms, "samp", scatter_dimension=0, tiled=True)
    local_genes = corr.shape[0]
    fold_onehot = (gene_folds[:, None] == jnp.arange(FOLDS)[None, :]).astype(jnp.float32)
    row_weights = jnp.dot(fold_onehot, fold_weights, precision=lax.Precision.HIGHEST)
    bin_match = distance_bins.T[:, :, None] == jnp.arange(NBINS)[None, None, :]
    tile_weight = jnp.sum(jnp.where(bin_match, row_weights[:, None, :], 0.0), axis=2)
    dof = jnp.float32(samples - COVS - 2)
    stats = dof * corr * corr
    weighted = stats.reshape(local_genes, VTILES, VTILE) * tile_weight[:, :, None]
    return weighted.reshape(local_genes, VARS)


def solution(mesh):
    return jax.shard_map(
        shards,
        mesh=mesh,
        in_specs=(
            P(("groups", "samp"), "var"),
            P(("groups", "samp"), "var"),
            P(("groups", "samp"), None),
            P("groups", ("var", "samp")),
            P(("groups", "var", "samp")),
            P(),
        ),
        out_specs=P(("groups", "var", "samp"), None),
        check_vma=False,
    )
```

profile of v0, /device:TPU:0, one launch (start us, length us, event | category | flops | bytes accessed | tf_op | source)
XLA Modules:
  0.0 191.9 jit_solution(71797673533566679)
XLA Ops:
  6.5 0.7 all-gather.2.cloned.1.call-update
  7.3 0.0 all-reduce.5.cloned.1.call-start
  7.3 1.2 fusion.11
  8.5 13.2 %psum.35 = f32[65,65]{0,1:T(8,128)S(1)} all-reduce(f32[65,65]{0,1:T(8,128)S(1)} %fusion.11), channel_id=1, replica_groups=mesh['groups'=1,'samp'=4,'var'=8] {'samp'}, use_global_device_ids=true, to_apply=%region_0.0 | all-reduce | flops 4225 | bytes 33800 | tf_op jit(solution)/shard_map/psum | solution.py:29
  21.7 0.1 copy.23
  21.8 5.9 %cholesky.16 = f32[65,65]{1,0:T(8,128)S(1)} custom-call(f32[65,65]{1,0:T(8,128)S(1)} %fusion.24), custom_call_target="Cholesky" | custom-call | tf_op jit(solution)/shard_map/jit(cholesky)/cholesky | solution.py:31
  27.8 2.4 %fusion.9 = f32[65,640]{1,0:T(8,128)} fusion(bf16[1024,640]{1,0:T(8,128)(2,1)} %param.6, bf16[1024,64]{0,1:T(8,128)(2,1)} %param.8), kind=kOutput, calls=%fused_computation.18 | convolution fusion | flops 85196800 | bytes 1608192 | tf_op jit(solution)/shard_map/dot_general | solution.py:26
  30.2 42.2 %all-gather.2.cloned.1.call-done = bf16[1024,1536]{0,1:T(8,128)(2,1)} async-done(((bf16[1024,192]{0,1:T(8,128)(2,1)}), bf16[1024,1536]{0,1:T(8,128)(2,1)}) %all-gather.2.cloned.1.call-update) | async-done | bytes 3145744 | tf_op jit(solution)/shard_map/all_gather | solution.py:24
  72.4 4.0 %fusion.5 = f32[65,1536]{1,0:T(8,128)} fusion(bf16[1024,1536]{0,1:T(8,128)(2,1)} %all-gather.2.cloned.1.call-done, bf16[1024,64]{0,1:T(8,128)(2,1)} %param.8), kind=kOutput, calls=%fused_computation.14 | convolution fusion | flops 204472320 | bytes 3676160 | tf_op jit(solution)/shard_map/dot_general | solution.py:27
  76.3 0.0 reduce-scatter.2.cloned.1.call-start
  76.4 0.7 compare_reduce_fusion
  77.1 0.6 fusion.15
  77.7 5.0 %custom-call.16 = f32[1,65,65]{1,2,0:T(8,128)S(1)} custom-call(f32[1,65,65]{2,1,0:T(8,128)S(1)} %fusion.15), custom_call_target="InvertDiagBlocksLowerTriangular" | custom-call | tf_op jit(solution)/shard_map/jit(_cho_solve)/triangular_solve | solution.py:15
  82.7 3.0 %copy.24 = bf16[1024,1536]{1,0:T(8,128)(2,1)} copy(bf16[1024,1536]{0,1:T(8,128)(2,1)S(1)} %copy-done.1) | data formatting | bytes 6291456 | tf_op jit(solution)/shard_map/all_gather | solution.py:24
  85.7 23.3 %all-reduce.5.cloned.1.call-done = (f32[65,1536]{1,0:T(8,128)}, f32[65,640]{1,0:T(8,128)}) async-done(((f32[65,1536]{1,0:T(8,128)}, f32[65,640]{1,0:T(8,128)}), (f32[65,1536]{1,0:T(8,128)}, f32[65,640]{1,0:T(8,128)})) %all-reduce.5.cloned.1.call-update) | async-done | bytes 565776 | tf_op jit(solution)/shard_map/psum | solution.py:29
  108.9 1.6 fusion.18
  110.5 0.5 fusion.16
  111.1 1.4 fusion.22
  112.5 0.3 fusion.20
  112.9 3.0 %multiply_reduce_fusion.1 = (f32[640]{0:T(1024)S(1)}, f32[1024,640]{1,0:T(8,128)}) fusion(bf16[1024,640]{1,0:T(8,128)(2,1)S(1)} %copy-done.3, f32[65,640]{1,0:T(8,128)S(1)} %fusion.20, bf16[1024,64]{0,1:T(8,128)(2,1)S(1)} %copy-done.4), kind=kOutput, calls=%fused_computation.6 | convolution fusion | flops 513801600 | bytes 4232192 | tf_op jit(solution)/shard_map/dot_general | solution.py:16
  115.8 5.1 %multiply_reduce_fusion = (f32[1536]{0:T(1024)S(1)}, f32[1024,1536]{1,0:T(8,128)}) fusion(f32[65,1536]{1,0:T(8,128)S(1)} %fusion.16, bf16[1024,64]{0,1:T(8,128)(2,1)S(1)} %copy-done.4, bf16[1024,1536]{1,0:T(8,128)(2,1)S(1)} %copy-done.2), kind=kOutput, calls=%fused_computation.1 | convolution fusion | flops 1233123840 | bytes 9973760 | tf_op jit(solution)/shard_map/dot_general | solution.py:16
  120.9 10.3 %all-reduce.1 = (f32[1536]{0:T(1024)S(1)}, f32[640]{0:T(1024)S(1)}) all-reduce(f32[1536]{0:T(1024)S(1)} %get-tuple-element.9, f32[640]{0:T(1024)S(1)} %get-tuple-element.11), channel_id=1, replica_groups=mesh['groups'=1,'samp'=4,'var'=8] {'samp'}, use_global_device_ids=true, to_apply=%region_8.9 | all-reduce | flops 2176 | bytes 17408 | tf_op jit(solution)/shard_map/psum | solution.py:34
  131.2 7.9 %fusion = f32[640,1536]{1,0:T(8,128)} fusion(f32[1024,1536]{1,0:T(8,128)} %get-tuple-element.10, f32[1536]{0:T(1024)S(1)} %add_rsqrt_fusion, f32[1024,640]{1,0:T(8,128)} %get-tuple-element.12, bf16[1024,640]{1,0:T(8,128)(2,1)S(1)} %copy-done.3, f32[640]{0:T(1024)S(1)} %add_rsqrt_fusion.1), kind=kOutput, calls=%fused_computation.3 | convolution fusion | flops 2019033088 | bytes 14164480 | tf_op jit(solution)/shard_map/dot_general | solution.py:39
  139.1 0.6 copy-done.6
  139.8 0.2 fusion.13
  140.0 0.0 copy-done.5
  140.0 0.1 select_reduce_fusion
  140.1 0.1 copy.25
  140.2 0.6 mul.51
  140.8 0.5 mul.52
  141.3 41.7 %reduce-scatter.2.cloned.1.call-done = f32[160,1536]{1,0:T(8,128)} async-done(((f32[640,1536]{1,0:T(8,128)}), f32[160,1536]{1,0:T(8,128)}) %reduce-scatter.2.cloned.1.call-update) | async-done | bytes 983056 | tf_op jit(solution)/shard_map/reduce_scatter | solution.py:42
  183.0 2.3 %fusion.3 = f32[160,1536]{1,0:T(8,128)} fusion(f32[160,1536]{1,0:T(8,128)S(1)} %mul.52, f32[160,1536]{1,0:T(8,128)} %reduce-scatter.2.cloned.1.call-done), kind=kLoop, calls=%fused_computation.10 | loop fusion | flops 737280 | bytes 2949120 | tf_op jit(solution)/shard_map/mul | solution.py:50
  (19 shorter events, 0.1 us)
Async XLA Ops:
  6.5 132.6 %copy-start = (f32[5,16]{1,0:T(8,128)S(1)}, f32[5,16]{1,0:T(8,128)}, u32[]{:S(2)}) copy-start(f32[5,16]{1,0:T(8,128)} %param.11) | copy-start | bytes 964
  6.5 65.8 %all-gather.2.cloned.1.call-start = ((), (), s32[]{:S(2)}) async-start(), calls=%async_computation.1 | async-start | bytes 3538944 | tf_op jit(solution)/shard_map/all_gather | solution.py:24
  7.3 101.7 %all-reduce.5.cloned.1.call-start = ((), (), s32[]{:S(2)}) async-start(), calls=%async_computation.3 | async-start | bytes 1253376 | tf_op jit(solution)/shard_map/psum | solution.py:29
  72.4 10.3 %copy-start.1 = (bf16[1024,1536]{0,1:T(8,128)(2,1)S(1)}, bf16[1024,1536]{0,1:T(8,128)(2,1)}, u32[]{:S(2)}) copy-start(bf16[1024,1536]{0,1:T(8,128)(2,1)} %all-gather.2.cloned.1.call-done) | copy-start | bytes 9437188
  76.3 106.7 %reduce-scatter.2.cloned.1.call-start = ((), (), s32[]{:S(2)}) async-start(), calls=%async_computation.2 | async-start | bytes 4915200 | tf_op jit(solution)/shard_map/reduce_scatter | solution.py:42
  85.7 27.2 %copy-start.3 = (bf16[1024,640]{1,0:T(8,128)(2,1)S(1)}, bf16[1024,640]{1,0:T(8,128)(2,1)}, u32[]{:S(2)}) copy-start(bf16[1024,640]{1,0:T(8,128)(2,1)} %param.6) | copy-start | bytes 3932164
  85.7 27.2 %copy-start.4 = (bf16[1024,64]{0,1:T(8,128)(2,1)S(1)}, bf16[1024,64]{0,1:T(8,128)(2,1)}, u32[]{:S(2)}) copy-start(bf16[1024,64]{0,1:T(8,128)(2,1)} %param.8) | copy-start | bytes 393220
  111.0 4.8 %copy-start.2 = (bf16[1024,1536]{1,0:T(8,128)(2,1)S(1)}, bf16[1024,1536]{1,0:T(8,128)(2,1)}, u32[]{:S(2)}) copy-start(bf16[1024,1536]{1,0:T(8,128)(2,1)} %copy.24) | copy-start | bytes 9437188
  139.1 0.7 copy-start.6
  139.1 0.9 copy-start.5
Sparse Core Ops, SparseCore 0:
  9.5 62.8 all-gather.1
  76.5 32.4 all-reduce.4
  139.2 43.7 reduce-scatter.1
where the time goes:
time: 192 us
  waiting for transfers between devices  108 us (56%)
  matrix products  27.5 us (14%)
  blocking collectives  23.5 us (12%)
  other arithmetic  14.7 us (8%)
  between operations  13.2 us (7%)
  local copies, waits for them, and re-layouts  4.89 us (3%)
    all_gather x1, waiting for transfers between devices, shards(): source = lax.all_gather(genotypes, 'var', axis=1, tiled=True)  42.2 us
    reduce_scatter x1, waiting for transfers between devices, shards(): corr = lax.psum_scatter(terms, 'samp', scatter_dimension=0, tiled=True)  41.7 us
    psum x1, waiting for transfers between devices, shards(): lax.psum((partial_sums[0], partial_sums[1], partial_sums[2]), 'samp')  23.3 us
    psum x1, blocking collectives, shards(): lax.psum((partial_sums[0], partial_sums[1], partial_sums[2]), 'samp')  13.2 us
    psum x1, blocking collectives, shards(): lax.psum((jnp.sum(expr_resid * expr_resid, axis=0), jnp.sum(geno_resid *...  10.3 us
    dot_general x2, matrix products, solve_fit(): jnp.dot(design.astype(jnp.float32), beta, precision=lax.Precision.HIGHEST)  8.05 us
    dot_general x1, matrix products, shards(): lax.dot_general(expr_unit, geno_unit, (((0,), (0,)), ((), ())), preferred...  7.86 us
    another operation x3, other arithmetic, shards(): factor = jnp.linalg.cholesky(gram)  6.64 us
  transfers between devices with their start and end apart: 3, of which 3 were waited for; matrix products, arithmetic and copies ran while one was open for 11% of the time, Pallas kernels for 0%

commit v1 on v0

--- a/solution.py
+++ b/solution.py
@@ -21,7 +21,8 @@
     sample_rows = expression.shape[0]
     samples = sample_rows * lax.axis_size("samp")
     design = jnp.concatenate([jnp.ones((sample_rows, 1), jnp.bfloat16), covariates], axis=1)
-    source = lax.all_gather(genotypes, "var", axis=1, tiled=True)
+    outgoing = jnp.stack([genotypes] * lax.axis_size("var"))
+    source = jnp.concatenate(lax.all_to_all(outgoing, "var", 0, 0), axis=1)
     gram = jnp.dot(design.T, design, preferred_element_type=jnp.float32)
     expr_cross = jnp.dot(design.T, expression, preferred_element_type=jnp.float32)
     geno_cross = jnp.dot(design.T, source, preferred_element_type=jnp.float32)

time: 192 us -> 206 us (1.073)
  starting transfers between devices: 0.08 us -> 7.52 us
  waiting for transfers between devices: 108 us -> 115 us
  matrix products: 27.5 us -> 24.4 us
  local copies, waits for them, and re-layouts: 4.89 us -> 7.96 us
    all_to_all x0 -> x1, waiting for transfers between devices: none -> 50.4 us  [shards(): source = jnp.concatenate(lax.all_to_all(outgoing, 'var', 0, 0), axis=1)]
    all_gather x1 -> x0, waiting for transfers between devices: 42.2 us -> none  [shards(): source = lax.all_gather(genotypes, 'var', axis=1, tiled=True)]
    all_to_all x0 -> x1, starting transfers between devices: none -> 7.44 us  [shards(): source = jnp.concatenate(lax.all_to_all(outgoing, 'var', 0, 0), axis=1)]
    another operation x0 -> x1, local copies, waits for them, and re-layouts: none -> 3.07 us  [shards(): outgoing = jnp.stack([genotypes] * lax.axis_size('var'))]
    all_gather x1 -> x0, local copies, waits for them, and re-layouts: 2.97 us -> none  [shards(): source = lax.all_gather(genotypes, 'var', axis=1, tiled=True)]
    reshape x0 -> x1, local copies, waits for them, and re-layouts: none -> 2.97 us  [shards(): source = jnp.concatenate(lax.all_to_all(outgoing, 'var', 0, 0), axis=1)]
    dot_general x1, matrix products: 3.95 us -> 1.85 us  [shards(): geno_cross = jnp.dot(design.T, source, preferred_element_type=jnp.float32)]
  transfers between devices with their start and end apart: 3 -> 3, of which waited for: 3 -> 3; matrix products, arithmetic and copies ran while one was open for 11% -> 9% of each run, Pallas kernels for 0% -> 0%
where the time goes in v1:
time: 206 us
  waiting for transfers between devices  115 us (56%)
  matrix products  24.4 us (12%)
  blocking collectives  22 us (11%)
  other arithmetic  14.9 us (7%)
  between operations  13.5 us (7%)
  local copies, waits for them, and re-layouts  7.96 us (4%)
  starting transfers between devices  7.52 us (4%)
    all_to_all x1, waiting for transfers between devices, shards(): source = jnp.concatenate(lax.all_to_all(outgoing, 'var', 0, 0), axis=1)  50.4 us
    reduce_scatter x1, waiting for transfers between devices, shards(): corr = lax.psum_scatter(terms, 'samp', scatter_dimension=0, tiled=True)  41.4 us
    psum x1, waiting for transfers between devices, shards(): lax.psum((partial_sums[0], partial_sums[1], partial_sums[2]), 'samp')  23.6 us
    psum x1, blocking collectives, shards(): lax.psum((partial_sums[0], partial_sums[1], partial_sums[2]), 'samp')  11.7 us
    psum x1, blocking collectives, shards(): lax.psum((jnp.sum(expr_resid * expr_resid, axis=0), jnp.sum(geno_resid *...  10.3 us
    dot_general x2, matrix products, solve_fit(): jnp.dot(design.astype(jnp.float32), beta, precision=lax.Precision.HIGHEST)  8.07 us
    dot_general x1, matrix products, shards(): lax.dot_general(expr_unit, geno_unit, (((0,), (0,)), ((), ())), preferred...  7.86 us
    all_to_all x1, starting transfers between devices, shards(): source = jnp.concatenate(lax.all_to_all(outgoing, 'var', 0, 0), axis=1)  7.44 us
  transfers between devices with their start and end apart: 3, of which 3 were waited for; matrix products, arithmetic and copies ran while one was open for 9% of the time, Pallas kernels for 0%

profile of v1, /device:TPU:0, one launch (start us, length us, event | category | flops | bytes accessed | tf_op | source)
XLA Modules:
  0.0 205.6 jit_solution(16160813606714416573)
XLA Ops:
  6.5 3.1 %stack.2 = bf16[8,1024,192]{1,2,0:T(8,128)(2,1)} broadcast(bf16[1024,192]{0,1:T(8,128)(2,1)} %param.7), dimensions={1,2} | broadcast | bytes 3538944 | tf_op jit(solution)/shard_map/stack | solution.py:24
  9.6 7.4 %all-to-all-start = ((bf16[8,1024,192]{1,2,0:T(8,128)(2,1)}), bf16[8,1024,192]{1,2,0:T(8,128)(2,1)S(1)}, u32[]{:S(2)}, u32[]{:S(2)}) async-start(bf16[8,1024,192]{1,2,0:T(8,128)(2,1)} %stack.2), calls=%async_computation | async-start | bytes 6291456 | tf_op jit(solution)/shard_map/all_to_all | solution.py:25
  17.1 0.0 all-reduce.5.cloned.1.call-start
  17.1 0.2 fusion.11
  17.3 11.7 %psum.35 = f32[65,65]{0,1:T(8,128)S(1)} all-reduce(f32[65,65]{0,1:T(8,128)S(1)} %fusion.11), channel_id=1, replica_groups=mesh['groups'=1,'samp'=4,'var'=8] {'samp'}, use_global_device_ids=true, to_apply=%region_0.0 | all-reduce | flops 4225 | bytes 33800 | tf_op jit(solution)/shard_map/psum | solution.py:30
  29.0 0.1 copy.18
  29.1 5.9 %cholesky.16 = f32[65,65]{1,0:T(8,128)S(1)} custom-call(f32[65,65]{1,0:T(8,128)S(1)} %fusion.24), custom_call_target="Cholesky" | custom-call | tf_op jit(solution)/shard_map/jit(cholesky)/cholesky | solution.py:32
  35.1 2.3 %fusion.9 = f32[65,640]{1,0:T(8,128)} fusion(bf16[1024,640]{1,0:T(8,128)(2,1)} %param.6, bf16[1024,64]{0,1:T(8,128)(2,1)S(1)} %copy-done.3), kind=kOutput, calls=%fused_computation.18 | convolution fusion | flops 85196800 | bytes 1608192 | tf_op jit(solution)/shard_map/dot_general | solution.py:27
  37.4 50.4 %all-to-all-done = bf16[8,1024,192]{1,2,0:T(8,128)(2,1)S(1)} async-done(((bf16[8,1024,192]{1,2,0:T(8,128)(2,1)}), bf16[8,1024,192]{1,2,0:T(8,128)(2,1)S(1)}, u32[]{:S(2)}, u32[]{:S(2)}) %all-to-all-start) | async-done | bytes 3145760 | tf_op jit(solution)/shard_map/all_to_all | solution.py:25
  87.8 1.9 fusion.5
  89.6 0.0 reduce-scatter.2.cloned.1.call-start
  89.7 0.7 compare_reduce_fusion
  90.4 0.7 fusion.15
  91.1 5.0 %custom-call.16 = f32[1,65,65]{1,2,0:T(8,128)S(1)} custom-call(f32[1,65,65]{2,1,0:T(8,128)S(1)} %fusion.15), custom_call_target="InvertDiagBlocksLowerTriangular" | custom-call | tf_op jit(solution)/shard_map/jit(_cho_solve)/triangular_solve | solution.py:15
  96.1 3.0 %copy.19 = bf16[1024,1536]{1,0:T(8,128)(2,1)} copy(bf16[1024,1536]{0,1:T(8,128)(2,1)S(1)} %bitcast.29) | data formatting | bytes 6291456 | tf_op jit(solution)/shard_map/reshape | solution.py:25
  99.1 23.6 %all-reduce.5.cloned.1.call-done = (f32[65,1536]{1,0:T(8,128)}, f32[65,640]{1,0:T(8,128)}) async-done(((f32[65,1536]{1,0:T(8,128)}, f32[65,640]{1,0:T(8,128)}), (f32[65,1536]{1,0:T(8,128)}, f32[65,640]{1,0:T(8,128)})) %all-reduce.5.cloned.1.call-update) | async-done | bytes 565776 | tf_op jit(solution)/shard_map/psum | solution.py:30
  122.7 1.6 fusion.18
  124.3 0.5 fusion.16
  124.8 1.4 fusion.22
  126.3 0.3 fusion.20
  126.6 3.0 %multiply_reduce_fusion.1 = (f32[640]{0:T(1024)S(1)}, f32[1024,640]{1,0:T(8,128)}) fusion(bf16[1024,640]{1,0:T(8,128)(2,1)S(1)} %copy-done.2, f32[65,640]{1,0:T(8,128)S(1)} %fusion.20, bf16[1024,64]{0,1:T(8,128)(2,1)S(1)} %copy-done.3), kind=kOutput, calls=%fused_computation.6 | convolution fusion | flops 513801600 | bytes 4232192 | tf_op jit(solution)/shard_map/dot_general | solution.py:16
  129.6 5.1 %multiply_reduce_fusion = (f32[1536]{0:T(1024)S(1)}, f32[1024,1536]{1,0:T(8,128)}) fusion(f32[65,1536]{1,0:T(8,128)S(1)} %fusion.16, bf16[1024,64]{0,1:T(8,128)(2,1)S(1)} %copy-done.3, bf16[1024,1536]{1,0:T(8,128)(2,1)S(1)} %copy-done.1), kind=kOutput, calls=%fused_computation.1 | convolution fusion | flops 1233123840 | bytes 9973760 | tf_op jit(solution)/shard_map/dot_general | solution.py:16
  134.7 10.3 %all-reduce.1 = (f32[1536]{0:T(1024)S(1)}, f32[640]{0:T(1024)S(1)}) all-reduce(f32[1536]{0:T(1024)S(1)} %get-tuple-element.9, f32[640]{0:T(1024)S(1)} %get-tuple-element.11), channel_id=1, replica_groups=mesh['groups'=1,'samp'=4,'var'=8] {'samp'}, use_global_device_ids=true, to_apply=%region_8.9 | all-reduce | flops 2176 | bytes 17408 | tf_op jit(solution)/shard_map/psum | solution.py:35
  145.0 7.9 %fusion = f32[640,1536]{1,0:T(8,128)} fusion(f32[1024,1536]{1,0:T(8,128)} %get-tuple-element.10, f32[1536]{0:T(1024)S(1)} %add_rsqrt_fusion, f32[1024,640]{1,0:T(8,128)} %get-tuple-element.12, bf16[1024,640]{1,0:T(8,128)(2,1)S(1)} %copy-done.2, f32[640]{0:T(1024)S(1)} %add_rsqrt_fusion.1), kind=kOutput, calls=%fused_computation.3 | convolution fusion | flops 2019033088 | bytes 14164480 | tf_op jit(solution)/shard_map/dot_general | solution.py:40
  152.9 0.6 copy-done.5
  153.5 0.2 fusion.13
  153.8 0.1 select_reduce_fusion
  153.9 0.1 copy.20
  154.0 0.6 mul.51
  154.6 0.5 mul.52
  155.1 41.4 %reduce-scatter.2.cloned.1.call-done = f32[160,1536]{1,0:T(8,128)} async-done(((f32[640,1536]{1,0:T(8,128)}), f32[160,1536]{1,0:T(8,128)}) %reduce-scatter.2.cloned.1.call-update) | async-done | bytes 983056 | tf_op jit(solution)/shard_map/reduce_scatter | solution.py:43
  196.4 2.3 %fusion.3 = f32[160,1536]{1,0:T(8,128)} fusion(f32[160,1536]{1,0:T(8,128)S(1)} %mul.52, f32[160,1536]{1,0:T(8,128)} %reduce-scatter.2.cloned.1.call-done), kind=kLoop, calls=%fused_computation.10 | loop fusion | flops 737280 | bytes 2949120 | tf_op jit(solution)/shard_map/mul | solution.py:51
  (17 shorter events, 0.1 us)
Async XLA Ops:
  6.5 146.4 %copy-start = (f32[5,16]{1,0:T(8,128)S(1)}, f32[5,16]{1,0:T(8,128)}, u32[]{:S(2)}) copy-start(f32[5,16]{1,0:T(8,128)} %param.11) | copy-start | bytes 964
  9.6 7.5 %copy-start.3 = (bf16[1024,64]{0,1:T(8,128)(2,1)S(1)}, bf16[1024,64]{0,1:T(8,128)(2,1)}, u32[]{:S(2)}) copy-start(bf16[1024,64]{0,1:T(8,128)(2,1)} %param.8) | copy-start | bytes 393220
  9.6 78.2 %all-to-all-start = ((bf16[8,1024,192]{1,2,0:T(8,128)(2,1)}), bf16[8,1024,192]{1,2,0:T(8,128)(2,1)S(1)}, u32[]{:S(2)}, u32[]{:S(2)}) async-start(bf16[8,1024,192]{1,2,0:T(8,128)(2,1)} %stack.2), calls=%async_computation | async-start | bytes 6291456 | tf_op jit(solution)/shard_map/all_to_all | solution.py:25
  17.1 105.7 %all-reduce.5.cloned.1.call-start = ((), (), s32[]{:S(2)}) async-start(), calls=%async_computation.3 | async-start | bytes 1253376 | tf_op jit(solution)/shard_map/psum | solution.py:30
  89.6 106.8 %reduce-scatter.2.cloned.1.call-start = ((), (), s32[]{:S(2)}) async-start(), calls=%async_computation.2 | async-start | bytes 4915200 | tf_op jit(solution)/shard_map/reduce_scatter | solution.py:43
  99.1 27.5 %copy-start.2 = (bf16[1024,640]{1,0:T(8,128)(2,1)S(1)}, bf16[1024,640]{1,0:T(8,128)(2,1)}, u32[]{:S(2)}) copy-start(bf16[1024,640]{1,0:T(8,128)(2,1)} %param.6) | copy-start | bytes 3932164
  124.8 4.8 %copy-start.1 = (bf16[1024,1536]{1,0:T(8,128)(2,1)S(1)}, bf16[1024,1536]{1,0:T(8,128)(2,1)}, u32[]{:S(2)}) copy-start(bf16[1024,1536]{1,0:T(8,128)(2,1)} %copy.19) | copy-start | bytes 9437188
  152.9 0.7 copy-start.5
  152.9 0.9 copy-start.4
Sparse Core Ops, SparseCore 0:
  89.8 32.9 all-reduce.4
  153.0 43.3 reduce-scatter.1
